TPU v7x, 32 devices: a whole 2x2x4 slice. The times are simulated.
32 devices in a mesh: row: 8 (over z, core), rep: 4 (over y, x).
Axes of the slice: x: 2, y: 2, z: 4, core: 2. Of those that a mesh axis runs over, the one named last changes fastest.
Arguments:
- features: bfloat16 [4096, 256], P(('row', 'rep')), may hold values from -6 to 6
- weight: bfloat16 [256, 256], replicated, may hold values from -0.375 to 0.375
- cotangent: bfloat16 [4096, 256], P(('row', 'rep')), may hold values from -6 to 6
- adjacency: bfloat16 [8, 4, 24, 128, 128], P('row', 'rep'), may hold values from -0.15625 to 0.15625
- tile_out: int32 [8, 4, 24], P('row', 'rep'), may hold values from 0 to 3
- tile_in: int32 [8, 4, 24], P('row', 'rep'), may hold values from 0 to 7
- live_count: int32 [8, 4], P('row', 'rep'), may hold values from 6 to 24, as said below
Outputs:
- activated: bfloat16 [4096, 256], P(('row', 'rep'))
- weight_grad: float32 [256, 256], replicated
- feature_grad: float32 [4096, 256], P(('row', 'rep'))
Inputs may be any that keep to these rules, and one draw needn't show every extreme that they name: `live_count`: live tile slots of one device; some device has all 24 slots live in every draw.
All inputs are finite; a program needn't handle non-finite values.
Results may differ from a plain program's by a relative error of at most 0.02.
Values may be sent and summed in bfloat16 or wider, within the bound.
A program may use at most 64 MiB of HBM per device.

v0:
```python
import math
import jax
import jax.numpy as jnp
from jax import lax
from jax.sharding import PartitionSpec as P


def tile_sums(adjacency, first_ids, second_ids, live_mask, table, count, transpose_tile):
    slot_count = adjacency.shape[0]
    block_rows = adjacency.shape[1]
    feat_width = table.shape[2]
    group_size = math.gcd(slot_count, 8)
    turns = slot_count // group_size
    items = (
        adjacency.reshape(turns, group_size, block_rows, block_rows),
        first_ids.reshape(turns, group_size),
        second_ids.reshape(turns, group_size),
        live_mask.reshape(turns, group_size),
    )

    def step_group(running, item):
        tile_group, read_ids, write_ids, live_group = item
        inputs = table[read_ids]
        if transpose_tile:
            products = jnp.einsum(
                "gji,gjf->gif", tile_group, inputs, preferred_element_type=jnp.float32
            )
        else:
            products = jnp.einsum(
                "gij,gjf->gif", tile_group, inputs, preferred_element_type=jnp.float32
            )
        onehot = (write_ids[None, :] == jnp.arange(count)[:, None]).astype(
            jnp.float32
        ) * live_group[None, :]
        running = running + jnp.einsum(
            "bg,gif->bif", onehot, products, precision=lax.Precision.HIGHEST
        )
        return (running, None)

    start = jnp.zeros((count, block_rows, feat_width), jnp.float32)
    running, unused = lax.scan(step_group, start, items)
    return running.reshape(count * block_rows, feat_width)


def add_sources(received):
    return jnp.sum(received.astype(jnp.float32), axis=0)


def body(features, weight, cotangent, adjacency, tile_out, tile_in, live_count):
    block_rows = features.shape[0]
    feat_width = features.shape[1]
    row_count = lax.axis_size("row")
    rep_count = lax.axis_size("rep")
    slot_count = adjacency.shape[2]
    adjacency = adjacency.reshape(slot_count, block_rows, block_rows)
    out_ids = tile_out.reshape(slot_count)
    in_ids = tile_in.reshape(slot_count)
    live_mask = (jnp.arange(slot_count) < live_count.reshape(())).astype(jnp.float32)
    gathered = lax.all_gather(features, "row", axis=0, tiled=True).reshape(
        row_count, block_rows, feat_width
    )
    partial_value = tile_sums(adjacency, in_ids, out_ids, live_mask, gathered, rep_count, False)
    aggregated = lax.psum_scatter(
        partial_value.astype(jnp.bfloat16), "rep", scatter_dimension=0, tiled=True
    )
    pre = jnp.dot(aggregated, weight, preferred_element_type=jnp.float32)
    sig = jax.nn.sigmoid(pre)
    activated = (pre * sig).astype(jnp.bfloat16)
    grad_pre = (cotangent.astype(jnp.float32) * sig * (1.0 + pre * (1.0 - sig))).astype(
        jnp.bfloat16
    )
    weight_part = jnp.dot(aggregated.T, grad_pre, preferred_element_type=jnp.float32)
    grad_rows = jnp.dot(grad_pre, weight.T, preferred_element_type=jnp.float32).astype(jnp.bfloat16)
    group_grads = lax.all_gather(grad_rows, "rep", axis=0, tiled=True)
    weight_grad = lax.psum(weight_part, ("row", "rep"))
    group_grads = group_grads.reshape(rep_count, block_rows, feat_width)
    returned = tile_sums(adjacency, out_ids, in_ids, live_mask, group_grads, row_count, True)
    rounded = returned.astype(jnp.bfloat16).reshape(row_count, block_rows, feat_width)
    feature_grad = add_sources(
        lax.all_to_all(rounded, "row", split_axis=0, concat_axis=0, tiled=True)
    )
    return (activated, weight_grad, feature_grad)


def solution(mesh):
    return jax.shard_map(
        body,
        mesh=mesh,
        in_specs=(
            P(("row", "rep"), None),
            P(),
            P(("row", "rep"), None),
            P("row", "rep", None, None, None),
            P("row", "rep", None),
            P("row", "rep", None),
            P("row", "rep"),
        ),
        out_specs=(P(("row", "rep"), None), P(), P(("row", "rep"), None)),
        check_vma=False,
    )
```

profile of v0, /device:TPU:0, one launch (start us, length us, event | category | flops | bytes accessed | tf_op | source)
XLA Modules:
  0.0 231.4 jit_solution(6620039171133740857)
XLA Ops:
  7.9 0.5 broadcast.99
  8.6 0.7 reduce.6
  9.3 0.7 reduce.7
  10.1 16.7 %all_gather.6 = bf16[1024,256]{1,0:T(8,128)(2,1)S(1)} all-gather(bf16[128,256]{1,0:T(8,128)(2,1)} %param.11), channel_id=1, replica_groups=mesh['row'=8,'rep'=4] {'row'}, dimensions={0}, use_global_device_ids=true | all-gather | bytes 589824 | tf_op jit(solution)/shard_map/all_gather | solution.py:59
  26.8 10.8 %while.22 = (s32[]{:T(128)}, f32[4,128,256]{2,0,1:T(4,128)S(1)}, s32[3,8]{1,0:T(4,128)S(1)}, f32[3,8]{1,0:T(4,128)S(1)}, bf16[3,8,128,128]{3,2,1,0:T(8,128)(2,1)...) while((s32[]{:T(128)}, f32[4,128,256]{2,0,1:T(4,128)S(1)}, ...), condition=%wide.region_1.2_spmd.clone, body=%wide.region_0.1_spmd.clone.sunk | while | flops 79955032 | bytes 4985279 | solution.py:41
  26.8 0.6 gather_fusion
  27.4 1.2 fusion.61
  28.7 1.7 convolution_add_fusion.4
  30.5 0.6 gather_fusion
  31.0 1.2 fusion.61
  32.3 1.7 convolution_add_fusion.4
  34.1 0.6 gather_fusion
  34.7 1.2 fusion.61
  35.9 1.7 convolution_add_fusion.4
  37.6 0.8 copy.25
  39.2 24.8 %reduce-scatter.2.cloned.1.call-done = bf16[128,256]{1,0:T(8,128)(2,1)} async-done(((bf16[512,256]{1,0:T(8,128)(2,1)}), bf16[128,256]{1,0:T(8,128)(2,1)}) %reduce-scatter.2.cloned.1.call-update) | async-done | bytes 65552 | tf_op jit(solution)/shard_map/reduce_scatter | solution.py:63
  64.0 1.7 multiply_convert_fusion
  65.9 9.3 %all_gather.7 = bf16[512,256]{1,0:T(8,128)(2,1)S(1)} all-gather(bf16[128,256]{1,0:T(8,128)(2,1)S(1)} %convolution_convert_fusion), channel_id=1, replica_groups=mesh['row'=8,'rep'=4] {'rep'}, dimensions={0}, use_global_device_ids=true | all-gather | bytes 327680 | tf_op jit(solution)/shard_map/all_gather | solution.py:74
  75.2 7.9 %while.23 = (s32[]{:T(128)}, f32[8,128,256]{2,0,1:T(8,128)S(1)}, s32[3,8]{1,0:T(4,128)S(1)}, f32[3,8]{1,0:T(4,128)S(1)}, bf16[3,8,128,128]{2,3,1,0:T(8,128)(2,1)...) while((s32[]{:T(128)}, f32[8,128,256]{2,0,1:T(8,128)S(1)}, ...), condition=%wide.region_5.6_spmd.clone, body=%wide.region_4.5_spmd.clone.sunk | while | flops 92800152 | bytes 6033855 | solution.py:41
  75.3 0.6 gather_fusion.1
  76.1 1.7 convolution_add_fusion.5
  77.9 0.6 gather_fusion.1
  78.8 1.7 convolution_add_fusion.5
  80.6 0.6 gather_fusion.1
  81.4 1.7 convolution_add_fusion.5
  83.1 1.1 copy.24
  84.2 4.8 %all-to-all-start = ((bf16[8,128,256]{2,1,0:T(8,128)(2,1)}), bf16[8,128,256]{2,1,0:T(8,128)(2,1)S(1)}, u32[]{:S(2)}, u32[]{:S(2)}) async-start(bf16[8,128,256]{2,1,0:T(8,128)(2,1)} %copy.24), calls=%async_computation.1 | async-start | bytes 1048576 | tf_op jit(solution)/shard_map/all_to_all | solution.py:80
  89.0 0.9 fusion.31
  90.0 14.4 %all-to-all-done = bf16[8,128,256]{2,1,0:T(8,128)(2,1)S(1)} async-done(((bf16[8,128,256]{2,1,0:T(8,128)(2,1)}), bf16[8,128,256]{2,1,0:T(8,128)(2,1)S(1)}, u32[]{:S(2)}, u32[]{:S(2)}) %all-to-all-start) | async-done | bytes 524320 | tf_op jit(solution)/shard_map/all_to_all | solution.py:80
  104.3 0.7 convert_reduce_fusion
  105.1 117.8 %all-reduce.2.cloned.1.call-done = f32[256,256]{1,0:T(8,128)} async-done(((f32[256,256]{1,0:T(8,128)}), f32[256,256]{1,0:T(8,128)}) %all-reduce.2.cloned.1.call-update) | async-done | bytes 262160 | tf_op jit(solution)/shard_map/psum | solution.py:75
  222.9 1.7 copy.44
  (50 shorter events, 2.5 us)
Async XLA Ops:
  7.2 56.8 %copy-start = (bf16[256,256]{1,0:T(8,128)(2,1)S(1)}, bf16[256,256]{1,0:T(8,128)(2,1)}, u32[]{:S(2)}) copy-start(bf16[256,256]{1,0:T(8,128)(2,1)} %param.12) | copy-start | bytes 393220
  7.2 56.8 %reduce-scatter.2.cloned.1.call-start = ((), (), s32[]{:S(2)}) async-start(), calls=%async_computation.2 | async-start | bytes 327680 | tf_op jit(solution)/shard_map/reduce_scatter | solution.py:63
  7.9 0.7 copy-start.4
  8.6 0.7 copy-start.5
  37.6 1.2 copy-start.1
  38.8 25.2 %copy-start.3 = (bf16[128,256]{1,0:T(8,128)(2,1)S(1)}, bf16[128,256]{1,0:T(8,128)(2,1)}, u32[]{:S(2)}) copy-start(bf16[128,256]{1,0:T(8,128)(2,1)} %param.13) | copy-start | bytes 196612
  84.2 4.8 %copy-start.2 = (bf16[128,256]{1,0:T(8,128)(2,1)S(1)}, bf16[128,256]{1,0:T(8,128)(2,1)}, u32[]{:S(2)}) copy-start(bf16[128,256]{1,0:T(8,128)(2,1)} %reduce-scatter.2.cloned.1.call-done) | copy-start | bytes 196612
  84.2 20.1 %all-to-all-start = ((bf16[8,128,256]{2,1,0:T(8,128)(2,1)}), bf16[8,128,256]{2,1,0:T(8,128)(2,1)S(1)}, u32[]{:S(2)}, u32[]{:S(2)}) async-start(bf16[8,128,256]{2,1,0:T(8,128)(2,1)} %copy.24), calls=%async_computation.1 | async-start | bytes 1048576 | tf_op jit(solution)/shard_map/all_to_all | solution.py:80
  89.0 133.9 %all-reduce.2.cloned.1.call-start = ((), (), s32[]{:S(2)}) async-start(), calls=%async_computation.3 | async-start | bytes 524288 | tf_op jit(solution)/shard_map/psum | solution.py:75
Sparse Core Ops, SparseCore 0:
  38.5 25.4 reduce-scatter.1
  95.9 126.9 all-reduce.1
where the time goes:
time: 232 us; the launch traced here: 231 us
  waiting for transfers between devices  157 us (68%)
  blocking collectives  26 us (11%)
  matrix products  17.5 us (8%)
  between operations  14.8 us (6%)
  local copies, waits for them, and re-layouts  8.77 us (4%)
  starting transfers between devices  4.83 us (2%)
    psum x1, waiting for transfers between devices, body(): weight_grad = lax.psum(weight_part, ('row', 'rep'))  118 us
    reduce_scatter x1, waiting for transfers between devices, body(): lax.psum_scatter(partial_value.astype(jnp.bfloat16), 'rep', scatter_dimen...  24.8 us
    all_gather x1, blocking collectives, body(): lax.all_gather(features, 'row', axis=0, tiled=True)  16.7 us
    all_to_all x1, waiting for transfers between devices, body(): lax.all_to_all(rounded, 'row', split_axis=0, concat_axis=0, tiled=True)  14.4 us
    dot_general x6, matrix products, step_group(): jnp.einsum('bg,gif->bif', onehot, products, precision=lax.Precision.HIGHEST)  10.2 us
    all_gather x1, blocking collectives, body(): group_grads = lax.all_gather(grad_rows, 'rep', axis=0, tiled=True)  9.29 us
    all_to_all x1, starting transfers between devices, body(): lax.all_to_all(rounded, 'row', split_axis=0, concat_axis=0, tiled=True)  4.75 us
  transfers between devices with their start and end apart: 3, of which 3 were waited for; matrix products, arithmetic and copies ran while one was open for 1% of the time, Pallas kernels for 0%

commit v1 on v0

--- a/solution.py
+++ b/solution.py
@@ -72,7 +72,8 @@
     weight_part = jnp.dot(aggregated.T, grad_pre, preferred_element_type=jnp.float32)
     grad_rows = jnp.dot(grad_pre, weight.T, preferred_element_type=jnp.float32).astype(jnp.bfloat16)
     group_grads = lax.all_gather(grad_rows, "rep", axis=0, tiled=True)
-    weight_grad = lax.psum(weight_part, ("row", "rep"))
+    parts = lax.all_gather(weight_part, ("row", "rep"))
+    weight_grad = jnp.sum(parts, axis=0)
     group_grads = group_grads.reshape(rep_count, block_rows, feat_width)
     returned = tile_sums(adjacency, out_ids, in_ids, live_mask, group_grads, row_count, True)
     rounded = returned.astype(jnp.bfloat16).reshape(row_count, block_rows, feat_width)

time: 232 us -> 166 us (0.72)
  waiting for transfers between devices: 157 us -> 58.4 us
  blocking collectives: 26 us -> 55 us
  other arithmetic: 2.17 us -> 8.09 us
  starting transfers between devices: 4.83 us -> 0.08 us
  matrix products: 17.5 us -> 21.2 us
    psum x1 -> x0, waiting for transfers between devices: 118 us -> none  [body(): weight_grad = lax.psum(weight_part, ('row', 'rep'))]
    all_gather x0 -> x1, waiting for transfers between devices: none -> 32.9 us  [body(): parts = lax.all_gather(weight_part, ('row', 'rep'))]
    all_to_all x0 -> x1, blocking collectives: none -> 28.2 us  [body(): lax.all_to_all(rounded, 'row', split_axis=0, concat_axis=0, tiled=True)]
    all_to_all x1 -> x0, waiting for transfers between devices: 14.4 us -> none  [body(): lax.all_to_all(rounded, 'row', split_axis=0, concat_axis=0, tiled=True)]
    all_to_all x1 -> x0, starting transfers between devices: 4.75 us -> none  [body(): lax.all_to_all(rounded, 'row', split_axis=0, concat_axis=0, tiled=True)]
    reduce_sum x0 -> x1, other arithmetic: none -> 4.63 us  [body(): weight_grad = jnp.sum(parts, axis=0)]
    dot_general x3, matrix products: 0.85 us -> 3.71 us  [step_group(): jnp.einsum('gji,gjf->gif', tile_group, inputs, preferred_element_type=jnp...]
  transfers between devices with their start and end apart: 3 -> 2, of which waited for: 3 -> 2; matrix products, arithmetic and copies ran while one was open for 1% -> 9% of each run, Pallas kernels for 0% -> 0%
where the time goes in v1:
time: 166 us
  waiting for transfers between devices  58.4 us (35%)
  blocking collectives  55 us (33%)
  matrix products  21.2 us (13%)
  between operations  14.8 us (9%)
  other arithmetic  8.09 us (5%)
  local copies, waits for them, and re-layouts  7.7 us (5%)
    all_gather x1, waiting for transfers between devices, body(): parts = lax.all_gather(weight_part, ('row', 'rep'))  32.9 us
    all_to_all x1, blocking collectives, body(): lax.all_to_all(rounded, 'row', split_axis=0, concat_axis=0, tiled=True)  28.2 us
    reduce_scatter x1, waiting for transfers between devices, body(): lax.psum_scatter(partial_value.astype(jnp.bfloat16), 'rep', scatter_dimen...  25.5 us
    all_gather x1, blocking collectives, body(): lax.all_gather(features, 'row', axis=0, tiled=True)  16.7 us
    dot_general x6, matrix products, step_group(): jnp.einsum('bg,gif->bif', onehot, products, precision=lax.Precision.HIGHEST)  10.2 us
    all_gather x1, blocking collectives, body(): group_grads = lax.all_gather(grad_rows, 'rep', axis=0, tiled=True)  10.1 us
    reduce_sum x1, other arithmetic, body(): weight_grad = jnp.sum(parts, axis=0)  4.63 us
    dot_general x3, matrix products, step_group(): jnp.einsum('gji,gjf->gif', tile_group, inputs, preferred_element_type=jnp...  3.71 us
  transfers between devices with their start and end apart: 2, of which 2 were waited for; matrix products, arithmetic and copies ran while one was open for 9% of the time, Pallas kernels for 0%

profile of v1, /device:TPU:0, one launch (start us, length us, event | category | flops | bytes accessed | tf_op | source)
XLA Modules:
  0.0 165.6 jit_solution(10340019128990848478)
XLA Ops:
  7.7 1.3 reduce.6
  9.8 1.3 reduce.7
  11.2 16.7 %all_gather.12 = bf16[1024,256]{1,0:T(8,128)(2,1)S(1)} all-gather(bf16[128,256]{1,0:T(8,128)(2,1)} %param.11), channel_id=1, replica_groups=mesh['row'=8,'rep'=4] {'row'}, dimensions={0}, use_global_device_ids=true | all-gather | bytes 589824 | tf_op jit(solution)/shard_map/all_gather | solution.py:59
  27.9 10.8 %while.22 = (s32[]{:T(128)}, f32[4,128,256]{2,0,1:T(4,128)S(1)}, s32[3,8]{1,0:T(4,128)S(1)}, f32[3,8]{1,0:T(4,128)S(1)}, bf16[3,8,128,128]{3,2,1,0:T(8,128)(2,1)...) while((s32[]{:T(128)}, f32[4,128,256]{2,0,1:T(4,128)S(1)}, ...), condition=%wide.region_1.2_spmd.clone, body=%wide.region_0.1_spmd.clone.sunk | while | flops 79955032 | bytes 4985279 | solution.py:41
  27.9 0.6 gather_fusion
  28.5 1.2 fusion.61
  29.8 1.7 %convolution_add_fusion.4 = f32[4,128,256]{2,0,1:T(4,128)S(1)} fusion(f32[8,128,256]{2,1,0:T(8,128)S(1)} %fusion.61, f32[4,128,256]{2,0,1:T(4,128)S(1)} %get-tuple-element.260, pred[]{:T(512)S(6)} %compare.6, f32[8]{0:T(128)S(1)} %fusion.62, s32[8]{0:T(128)S(1)} %fusion.63), kind=kOutput, calls=%fused_computation.2.clone.1 | convolution fusion | flops 12845120 | bytes 2097217 | tf_op jit(solution)/shard_map/while/body/eval_jaxpr/bg,gif->bif/dot_general | solution.py:35
  31.6 0.6 gather_fusion
  32.1 1.2 fusion.61
  33.4 1.7 %convolution_add_fusion.4 = f32[4,128,256]{2,0,1:T(4,128)S(1)} fusion(f32[8,128,256]{2,1,0:T(8,128)S(1)} %fusion.61, f32[4,128,256]{2,0,1:T(4,128)S(1)} %get-tuple-element.260, pred[]{:T(512)S(6)} %compare.6, f32[8]{0:T(128)S(1)} %fusion.62, s32[8]{0:T(128)S(1)} %fusion.63), kind=kOutput, calls=%fused_computation.2.clone.1 | convolution fusion | flops 12845120 | bytes 2097217 | tf_op jit(solution)/shard_map/while/body/eval_jaxpr/bg,gif->bif/dot_general | solution.py:35
  35.2 0.6 gather_fusion
  35.8 1.2 fusion.61
  37.0 1.7 %convolution_add_fusion.4 = f32[4,128,256]{2,0,1:T(4,128)S(1)} fusion(f32[8,128,256]{2,1,0:T(8,128)S(1)} %fusion.61, f32[4,128,256]{2,0,1:T(4,128)S(1)} %get-tuple-element.260, pred[]{:T(512)S(6)} %compare.6, f32[8]{0:T(128)S(1)} %fusion.62, s32[8]{0:T(128)S(1)} %fusion.63), kind=kOutput, calls=%fused_computation.2.clone.1 | convolution fusion | flops 12845120 | bytes 2097217 | tf_op jit(solution)/shard_map/while/body/eval_jaxpr/bg,gif->bif/dot_general | solution.py:35
  38.7 0.8 copy.25
  39.6 25.5 %reduce-scatter.2.cloned.1.call-done = bf16[128,256]{1,0:T(8,128)(2,1)} async-done(((bf16[512,256]{1,0:T(8,128)(2,1)}), bf16[128,256]{1,0:T(8,128)(2,1)}) %reduce-scatter.2.cloned.1.call-update) | async-done | bytes 65552 | tf_op jit(solution)/shard_map/reduce_scatter | solution.py:63
  65.1 1.7 %multiply_convert_fusion = (bf16[128,256]{1,0:T(8,128)(2,1)S(1)}, bf16[128,256]{1,0:T(8,128)(2,1)}) fusion(bf16[128,256]{1,0:T(8,128)(2,1)S(1)} %copy-done.1, bf16[128,256]{1,0:T(8,128)(2,1)} %reduce-scatter.2.cloned.1.call-done, bf16[256,256]{1,0:T(8,128)(2,1)S(1)} %copy-done), kind=kOutput, calls=%fused_computation.50 | convolution fusion | flops 17170432 | bytes 393216 | tf_op jit(solution)/shard_map/dot_general | solution.py:66
  66.8 1.8 %fusion.31 = f32[256,256]{1,0:T(8,128)} fusion(bf16[128,256]{1,0:T(8,128)(2,1)} %reduce-scatter.2.cloned.1.call-done, bf16[128,256]{1,0:T(8,128)(2,1)S(1)} %get-tuple-element.162), kind=kOutput, calls=%fused_computation.55 | convolution fusion | flops 16777216 | bytes 393216 | tf_op jit(solution)/shard_map/dot_general | solution.py:72
  68.6 2.3 %copy.13 = bf16[1,1,24,128,128]{3,4,2,1,0:T(8,128)(2,1)} copy(bf16[1,1,24,128,128]{4,3,2,1,0:T(8,128)(2,1)} %bitcast.84) | data formatting | bytes 1572864 | tf_op args[3]
  71.1 10.1 %all_gather.15 = bf16[512,256]{1,0:T(8,128)(2,1)S(1)} all-gather(bf16[128,256]{1,0:T(8,128)(2,1)S(1)} %convolution_convert_fusion), channel_id=1, replica_groups=mesh['row'=8,'rep'=4] {'rep'}, dimensions={0}, use_global_device_ids=true | all-gather | bytes 327680 | tf_op jit(solution)/shard_map/all_gather | solution.py:74
  81.3 10.8 %while.23 = (s32[]{:T(128)}, f32[8,128,256]{2,0,1:T(8,128)S(1)}, s32[3,8]{1,0:T(4,128)S(1)}, f32[3,8]{1,0:T(4,128)S(1)}, bf16[3,8,128,128]{2,3,1,0:T(8,128)(2,1)...) while((s32[]{:T(128)}, f32[8,128,256]{2,0,1:T(8,128)S(1)}, ...), condition=%wide.region_5.6_spmd.clone, body=%wide.region_4.5_spmd.clone.sunk | while | flops 92800152 | bytes 6033855 | solution.py:41
  81.3 0.6 gather_fusion.1
  81.9 1.2 fusion.69
  83.1 1.7 %convolution_add_fusion.5 = f32[8,128,256]{2,0,1:T(8,128)S(1)} fusion(f32[8,128,256]{2,1,0:T(8,128)S(1)} %fusion.69, f32[8,128,256]{2,0,1:T(8,128)S(1)} %get-tuple-element.287, pred[]{:T(512)S(6)} %compare.7, f32[8]{0:T(128)S(1)} %fusion.70, s32[8]{0:T(128)S(1)} %fusion.71), kind=kOutput, calls=%fused_computation.24.clone.1 | convolution fusion | flops 25690240 | bytes 3145793 | tf_op jit(solution)/shard_map/while/body/eval_jaxpr/bg,gif->bif/dot_general | solution.py:35
  84.9 0.6 gather_fusion.1
  85.5 1.2 fusion.69
  86.7 1.7 %convolution_add_fusion.5 = f32[8,128,256]{2,0,1:T(8,128)S(1)} fusion(f32[8,128,256]{2,1,0:T(8,128)S(1)} %fusion.69, f32[8,128,256]{2,0,1:T(8,128)S(1)} %get-tuple-element.287, pred[]{:T(512)S(6)} %compare.7, f32[8]{0:T(128)S(1)} %fusion.70, s32[8]{0:T(128)S(1)} %fusion.71), kind=kOutput, calls=%fused_computation.24.clone.1 | convolution fusion | flops 25690240 | bytes 3145793 | tf_op jit(solution)/shard_map/while/body/eval_jaxpr/bg,gif->bif/dot_general | solution.py:35
  89.1 1.2 fusion.69
  90.3 1.7 %convolution_add_fusion.5 = f32[8,128,256]{2,0,1:T(8,128)S(1)} fusion(f32[8,128,256]{2,1,0:T(8,128)S(1)} %fusion.69, f32[8,128,256]{2,0,1:T(8,128)S(1)} %get-tuple-element.287, pred[]{:T(512)S(6)} %compare.7, f32[8]{0:T(128)S(1)} %fusion.70, s32[8]{0:T(128)S(1)} %fusion.71), kind=kOutput, calls=%fused_computation.24.clone.1 | convolution fusion | flops 25690240 | bytes 3145793 | tf_op jit(solution)/shard_map/while/body/eval_jaxpr/bg,gif->bif/dot_general | solution.py:35
  92.3 28.2 %all_to_all.5 = bf16[8,128,256]{2,1,0:T(8,128)(2,1)S(1)} all-to-all(bf16[8,128,256]{2,1,0:T(8,128)(2,1)S(1)} %copy.24), channel_id=1, replica_groups=mesh['row'=8,'rep'=4] {'row'}, dimensions={0} | all-to-all | bytes 1048576 | tf_op jit(solution)/shard_map/all_to_all | solution.py:81
  120.5 0.7 convert_reduce_fusion
  121.2 32.9 %all-gather.3.cloned.1.call-done = f32[8192,256]{1,0:T(8,128)} async-done(((f32[256,256]{1,0:T(8,128)}), f32[8192,256]{1,0:T(8,128)}) %all-gather.3.cloned.1.call-update) | async-done | bytes 8388624 | tf_op jit(solution)/shard_map/all_gather | solution.py:75
  154.1 4.6 %reduce_sum.18 = f32[256,256]{1,0:T(8,128)} reduce(f32[32,256,256]{2,1,0:T(8,128)} %bitcast.82, f32[]{:T(128)} %constant.38.clone.1), dimensions={0}, to_apply=%region_3.4 | reduce | flops 2031616 | bytes 8650756 | tf_op jit(solution)/shard_map/reduce_sum | solution.py:76
  (41 shorter events, 2.1 us)
Async XLA Ops:
  7.2 58.0 %copy-start = (bf16[256,256]{1,0:T(8,128)(2,1)S(1)}, bf16[256,256]{1,0:T(8,128)(2,1)}, u32[]{:S(2)}) copy-start(bf16[256,256]{1,0:T(8,128)(2,1)} %param.12) | copy-start | bytes 393220
  7.2 57.9 %reduce-scatter.2.cloned.1.call-start = ((), (), s32[]{:S(2)}) async-start(), calls=%async_computation.2 | async-start | bytes 327680 | tf_op jit(solution)/shard_map/reduce_scatter | solution.py:63
  27.9 37.2 %copy-start.1 = (bf16[128,256]{1,0:T(8,128)(2,1)S(1)}, bf16[128,256]{1,0:T(8,128)(2,1)}, u32[]{:S(2)}) copy-start(bf16[128,256]{1,0:T(8,128)(2,1)} %param.13) | copy-start | bytes 196612
  39.6 114.5 %all-gather.3.cloned.1.call-start = ((), (), s32[]{:S(2)}) async-start(), calls=%async_computation.3 | async-start | bytes 8650752 | tf_op jit(solution)/shard_map/all_gather | solution.py:75
Sparse Core Ops, SparseCore 0:
  39.7 25.4 reduce-scatter.1
  68.7 85.3 all-gather.2
